TPU v7x, 128 devices: a whole 4x4x4 slice. The times are simulated.
128 devices in a mesh: ctx: 16 (over y_lo, z, core), head: 8 (over y_hi, x).
Axes of the slice: x: 4, y: 4 (y_hi: 2, y_lo: 2; y = y_hi * 2 + y_lo), z: 4, core: 2. Of those that a mesh axis runs over, the one named last changes fastest.
Arguments:
- queries: bfloat16 [16384, 4096], P('ctx', 'head'), may hold values from -8 to 8
- keys: bfloat16 [16384, 1024], P('ctx', 'head'), may hold values from -8 to 8
Outputs:
- grad_queries: float32 [16384, 4096], P('ctx', 'head')
- grad_blocks: float32 [32, 1024], P('ctx', 'head')
- loss: float32 [], replicated
All inputs are finite; a program needn't handle non-finite values.
Results may differ from a plain program's by a relative error of at most 0.00045.
Values may be sent and summed in bfloat16 or wider, within the bound.
A program may use at most 64 MiB of HBM per device.

v0:
```python
import functools
import math

import jax
import jax.numpy as jnp
from jax import lax
from jax.sharding import PartitionSpec as P

D_HEAD = 128
HEADS = 32
KV_HEADS = 8
BLOCK = 512


NEG_FLOOR = -1e30


def advance_span(
    query_block, query_pos, key_rows, key_pos, block_slots, first_block, score_scale, span_state
):
    old_peak, old_mass = span_state
    scores = (
        jnp.einsum("qgrd,kgd->qgrk", query_block, key_rows, preferred_element_type=jnp.float32)
        * score_scale
    )
    causal_mask = key_pos[None, None, None, :] <= query_pos[:, None, None, None]
    new_peak = jnp.maximum(old_peak, jnp.max(jnp.where(causal_mask, scores, NEG_FLOOR), axis=-1))
    probability = jnp.where(causal_mask, jnp.exp(scores - new_peak[..., None]), 0.0)
    span_shape = probability.shape
    block_part = jnp.sum(
        probability.reshape(span_shape[0], span_shape[1], span_shape[2], block_slots, BLOCK),
        axis=-1,
    )
    shrunk = old_mass * jnp.exp(old_peak - new_peak)[..., None]
    current = lax.dynamic_slice_in_dim(shrunk, first_block, block_slots, 3)
    return (new_peak, lax.dynamic_update_slice_in_dim(shrunk, current + block_part, first_block, 3))


def unchanged(span_state):
    return span_state


def local(queries, keys):
    ctx_count = lax.axis_size("ctx")
    ctx_rank = lax.axis_index("ctx")
    tok_rows = queries.shape[0]
    kv_local = keys.shape[1] // D_HEAD
    group_size = HEADS // KV_HEADS
    seq_len = tok_rows * ctx_count
    block_count = seq_len // BLOCK
    score_scale = D_HEAD ** (-0.5)
    row_index = jnp.arange(tok_rows, dtype=jnp.int32)
    positions = ctx_rank * tok_rows + row_index
    query_heads = queries.reshape(tok_rows, kv_local, group_size, D_HEAD)
    query_span = min(tok_rows, 512)
    pad_blocks = 1024 // BLOCK + 2
    initial = (
        jnp.full((tok_rows, kv_local, group_size), NEG_FLOOR, jnp.float32),
        jnp.zeros((tok_rows, kv_local, group_size, block_count + pad_blocks), jnp.float32),
        jnp.zeros((block_count + pad_blocks, kv_local * D_HEAD), jnp.float32),
    )
    running = initial
    key_piece = lax.all_gather(keys, "ctx", axis=0, tiled=True)
    row_count = key_piece.shape[0]
    sub_rows = math.gcd(row_count, 1024)
    sub_steps = row_count // sub_rows
    block_slots = sub_rows // BLOCK
    key_parts = key_piece.reshape(sub_steps, sub_rows, kv_local, D_HEAD)
    part_starts = sub_rows * jnp.arange(sub_steps, dtype=jnp.int32)

    def absorb_part(scan_state, inputs):
        row_peak, block_mass, key_sums = scan_state
        key_rows, key_start = inputs
        key_pos = key_start + jnp.arange(sub_rows, dtype=jnp.int32)
        first_block = key_start // BLOCK
        peak_list = []
        mass_list = []
        for span_number in range(tok_rows // query_span):
            row_low = span_number * query_span
            query_block = query_heads[row_low : row_low + query_span]
            query_pos = positions[row_low : row_low + query_span]
            span_state = (
                row_peak[row_low : row_low + query_span],
                block_mass[row_low : row_low + query_span],
            )
            advance = functools.partial(
                advance_span,
                query_block,
                query_pos,
                key_rows,
                key_pos,
                block_slots,
                first_block,
                score_scale,
            )
            new_state = lax.cond(key_start <= jnp.max(query_pos), advance, unchanged, span_state)
            peak_list.append(new_state[0])
            mass_list.append(new_state[1])
        return ((jnp.concatenate(peak_list, 0), jnp.concatenate(mass_list, 0), key_sums), None)

    running, _ = lax.scan(absorb_part, running, (key_parts, part_starts))
    _, block_mass, key_sums = running
    block_mass = block_mass[..., :block_count]
    teacher = block_mass / jnp.sum(block_mass, axis=-1, keepdims=True)
    own_pooled = (
        jnp.sum(
            keys.reshape(tok_rows // BLOCK, BLOCK, kv_local * D_HEAD), axis=1, dtype=jnp.float32
        )
        / BLOCK
    )
    pooled = lax.all_gather(own_pooled, "ctx", axis=0, tiled=True)
    pooled_heads = pooled.reshape(block_count, kv_local, D_HEAD)
    query_float = query_heads.astype(jnp.float32)
    gate_logits = jnp.einsum(
        "qgrd,bgd->qgrb", query_float, pooled_heads, precision=lax.Precision.HIGHEST
    )
    allowed = (jnp.arange(block_count, dtype=jnp.int32)[None, :] <= (positions // BLOCK)[:, None])[
        :, None, None, :
    ]
    logit_peak = jnp.max(jnp.where(allowed, gate_logits, NEG_FLOOR), axis=-1, keepdims=True)
    weights = jnp.where(allowed, jnp.exp(gate_logits - logit_peak), 0.0)
    weight_sum = jnp.sum(weights, axis=-1, keepdims=True)
    student = weights / weight_sum
    cross_entropy = (
        logit_peak[..., 0] + jnp.log(weight_sum[..., 0]) - jnp.sum(teacher * gate_logits, axis=-1)
    )
    gate_error = student - teacher
    grad_rows = jnp.einsum(
        "qgrb,bgd->qgrd", gate_error, pooled_heads, precision=lax.Precision.HIGHEST
    ).reshape(tok_rows, kv_local * group_size * D_HEAD)
    summed = jnp.einsum("qgrb,qgrd->bgd", gate_error, query_float, precision=lax.Precision.HIGHEST)
    grad_blocks = lax.psum_scatter(
        summed.reshape(tok_rows // BLOCK * lax.axis_size("ctx"), kv_local * D_HEAD) / BLOCK,
        "ctx",
        scatter_dimension=0,
        tiled=True,
    )
    loss = lax.psum(jnp.sum(cross_entropy), ("ctx", "head")) / (seq_len * HEADS)
    return (grad_rows, grad_blocks, loss)


def solution(mesh):
    in_specs = (P("ctx", "head"), P("ctx", "head"))
    out_specs = (P("ctx", "head"), P("ctx", "head"), P())
    return jax.shard_map(local, mesh=mesh, in_specs=in_specs, out_specs=out_specs, check_vma=False)
```

profile of v0, /device:TPU:1, one launch (start us, length us, event | category | flops | bytes accessed | tf_op | source)
XLA Modules:
  0.0 690.9 jit_solution(7276196982096939368)
XLA Ops:
  13.0 22.3 %all-gather = f32[16,2,128]{2,1,0:T(2,128)S(1)} all-gather(f32[1,2,128]{2,1,0:T(2,128)S(1)} %multiply_bitcast_fusion), channel_id=1, replica_groups=mesh['ctx'=16,'head'=8] {'ctx'}, dimensions={0}, use_global_device_ids=true | all-gather | bytes 17408 | tf_op jit(solution)/shard_map/all_gather | solution.py:111
  36.1 2.4 select_reduce_fusion
  38.5 12.2 %all-gather.3.cloned.1.call-done = bf16[16384,128]{1,0:T(8,128)(2,1)} async-done(((bf16[1024,128]{1,0:T(8,128)(2,1)}), bf16[16384,128]{1,0:T(8,128)(2,1)}) %all-gather.3.cloned.1.call-update) | async-done | bytes 4194320 | tf_op jit(solution)/shard_map/all_gather | solution.py:63
  50.8 179.9 %while.15 = (s32[]{:T(128)}, f32[1024,1,4]{0,2,1:T(4,128)S(1)}, f32[1024,1,4,36]{0,2,3,1:T(4,128)S(1)}, s32[16]{0:T(128)S(1)}, s32[]{:T(128)}, /*index=5*/bf16[1...) while((s32[]{:T(128)}, f32[1024,1,4]{0,2,1:T(4,128)S(1)}, ...), condition=%wide.region_14.15_spmd.clone, body=%wide.region_5.14_spmd.clone.sunk | while | flops 1104455680 | bytes 78656088 | solution.py:101
  57.2 11.9 %conditional.7 = (f32[512,1,4]{0,2,1:T(4,128)S(1)}, f32[512,1,4,36]{0,2,3,1:T(4,128)S(1)}) conditional(s32[]{:T(128)} %convert_element_type.27, (f32[512,1,4]{0,2,1:T(4,128)S(1)}, f32[512,1,4,36]{0,3,2,1:T(8,128)S(1)}) %tuple.82, (s32[1024]{0:T(1024)S(1)}, s32[1024]{0:T(1024)S(1)}, bf16[1024,1,128]{2,0,1:T(8,128)(2,1)S(1)}, ...), branch_computations={%region_6.6_spmd, %region_7.9_spmd} | conditional | flops 552151040 | bytes 37259324 | solution.py:96
  57.6 2.0 fusion.2
  59.6 4.8 fusion.4
  64.4 4.2 reduce_sum.43
  70.4 11.9 %conditional.6 = (f32[512,1,4]{0,2,1:T(4,128)S(1)}, f32[512,1,4,36]{0,2,3,1:T(4,128)S(1)}) conditional(s32[]{:T(128)} %convert_element_type.26, (f32[512,1,4]{0,2,1:T(4,128)S(1)}, f32[512,1,4,36]{0,3,2,1:T(8,128)S(1)}) %tuple.80, (s32[1024]{0:T(1024)S(1)}, s32[1024]{0:T(1024)S(1)}, bf16[1024,1,128]{2,0,1:T(8,128)(2,1)S(1)}, ...), branch_computations={%region_10.10_spmd, %region_11.13_spmd} | conditional | flops 552151040 | bytes 37259324 | solution.py:96
  70.8 2.0 fusion.9
  72.8 4.8 fusion.11
  77.6 4.2 reduce_sum.60
  88.9 11.9 %conditional.7 = (f32[512,1,4]{0,2,1:T(4,128)S(1)}, f32[512,1,4,36]{0,2,3,1:T(4,128)S(1)}) conditional(s32[]{:T(128)} %convert_element_type.27, (f32[512,1,4]{0,2,1:T(4,128)S(1)}, f32[512,1,4,36]{0,3,2,1:T(8,128)S(1)}) %tuple.82, (s32[1024]{0:T(1024)S(1)}, s32[1024]{0:T(1024)S(1)}, bf16[1024,1,128]{2,0,1:T(8,128)(2,1)S(1)}, ...), branch_computations={%region_6.6_spmd, %region_7.9_spmd} | conditional | flops 552151040 | bytes 37259324 | solution.py:96
  89.3 2.0 fusion.2
  91.3 4.8 fusion.4
  96.1 4.2 reduce_sum.43
  102.0 11.9 %conditional.6 = (f32[512,1,4]{0,2,1:T(4,128)S(1)}, f32[512,1,4,36]{0,2,3,1:T(4,128)S(1)}) conditional(s32[]{:T(128)} %convert_element_type.26, (f32[512,1,4]{0,2,1:T(4,128)S(1)}, f32[512,1,4,36]{0,3,2,1:T(8,128)S(1)}) %tuple.80, (s32[1024]{0:T(1024)S(1)}, s32[1024]{0:T(1024)S(1)}, bf16[1024,1,128]{2,0,1:T(8,128)(2,1)S(1)}, ...), branch_computations={%region_10.10_spmd, %region_11.13_spmd} | conditional | flops 552151040 | bytes 37259324 | solution.py:96
  102.4 2.0 fusion.9
  104.5 4.8 fusion.11
  109.3 4.2 reduce_sum.60
  231.3 3.2 fusion.22
  237.0 391.8 %psum.7 = f32[]{:T(128)} all-reduce(f32[]{:T(128)} %subtract_reduce_fusion), channel_id=1, replica_groups=mesh['ctx'=16,'head'=8] {'ctx','head'}, use_global_device_ids=true, to_apply=%region_19.20 | all-reduce | flops 1 | bytes 8 | tf_op jit(solution)/shard_map/psum | solution.py:138
  628.9 49.9 %all-reduce = f32[32,128]{1,0:T(8,128)S(1)} all-reduce(f32[32,128]{1,0:T(8,128)S(1)} %fusion.16), channel_id=2, replica_groups=mesh['ctx'=16,'head'=8] {'ctx'}, use_global_device_ids=true, to_apply=%region_16.17.clone | all-reduce | flops 4096 | bytes 32768
  678.8 2.9 copy.28
  (232 shorter events, 69.4 us)
Async XLA Ops:
  7.2 43.5 %all-gather.3.cloned.1.call-start = ((), (), s32[]{:S(2)}) async-start(), calls=%async_computation | async-start | bytes 4456448 | tf_op jit(solution)/shard_map/all_gather | solution.py:63
Sparse Core Ops, SparseCore 0:
  9.7 40.9 all-gather.2
where the time goes:
time: 697 us; the launch traced here: 691 us
  blocking collectives  464 us (67%)
  loops' own time  82.3 us (12%)
  other arithmetic  52.7 us (8%)
  local copies, waits for them, and re-layouts  46.8 us (7%)
  between operations  16.6 us (2%)
  matrix products  15.5 us (2%)
  waiting for transfers between devices  12.9 us (2%)
    psum x1, blocking collectives, local(): loss = lax.psum(jnp.sum(cross_entropy), ('ctx', 'head')) / (seq_len * HEADS)  392 us
    another operation x1, loops' own time, local(): running, _ = lax.scan(absorb_part, running, (key_parts, part_starts))  81.5 us
    unnamed x1, blocking collectives  49.9 us
    all_gather x1, blocking collectives, local(): pooled = lax.all_gather(own_pooled, 'ctx', axis=0, tiled=True)  22.3 us
    select_n x4, other arithmetic, advance_span(): jnp.where(causal_mask, jnp.exp(scores - new_peak[..., None]), 0.0)  19.1 us
    reduce_sum x4, other arithmetic, advance_span(): jnp.sum(probability.reshape(span_shape[0], span_shape[1], span_shape[2],...  16.7 us
    squeeze x16, local copies, waits for them, and re-layouts, local(): running, _ = lax.scan(absorb_part, running, (key_parts, part_starts))  15.6 us
  transfers between devices with their start and end apart: 1, of which 1 were waited for; matrix products, arithmetic and copies ran while one was open for 1% of the time, Pallas kernels for 0%

commit v1 on v0

v1 whole, which is shorter than its diff:
```python
import functools
import math

import jax
import jax.numpy as jnp
from jax import lax
from jax.experimental import pallas as pl
from jax.experimental.pallas import tpu as pltpu
from jax.sharding import PartitionSpec as P

D_HEAD = 128
HEADS = 32
KV_HEADS = 8
BLOCK = 512
GROUP = HEADS // KV_HEADS
NEG_FLOOR = -1e30
SCALE = D_HEAD ** (-0.5)
EXP2_SCALE = SCALE * math.log2(math.e)
TOTAL_LOW = 1e-25
TOTAL_HIGH = 3e38
MESH = pl.DeviceIdType.MESH
NT = (((1,), (1,)), ((), ()))
NN = (((1,), (0,)), ((), ()))
TN = (((0,), (0,)), ((), ()))
F32 = jnp.float32
BF16 = jnp.bfloat16


def split3(x):
    a = x.astype(BF16)
    rest = x - a.astype(F32)
    b = rest.astype(BF16)
    c = (rest - b.astype(F32)).astype(BF16)
    return a, b, c


def kernel(
    safe,
    n_ctx,
    n_head,
    q_hbm,
    k_hbm,
    gq_ref,
    gb_ref,
    st_ref,
    q_ref,
    kbuf,
    mass,
    peak,
    pool,
    parts,
    gbs,
    gbr,
    hsend,
    hrecv,
    loc_sem,
    own_send,
    fwd_send,
    key_recv,
    r1_send,
    r1_recv,
    r2_send,
    r2_recv,
):
    rank = lax.axis_index("ctx")
    head = lax.axis_index("head")
    chip = rank // 2
    core = rank % 2
    sibling = chip * 2 + 1 - core
    rows = q_ref.shape[0]
    n_chip = n_ctx // 2
    n_block = mass.shape[1]

    barrier = pltpu.get_barrier_semaphore()

    @pl.loop(1, n_ctx)
    def _(o):
        pl.semaphore_signal(
            barrier, inc=1, device_id={"ctx": lax.rem(rank + o, n_ctx)}, device_id_type=MESH
        )

    @pl.loop(1, n_head)
    def _(o):
        pl.semaphore_signal(
            barrier, inc=1, device_id={"head": lax.rem(head + o, n_head)}, device_id_type=MESH
        )

    q_copy = pltpu.make_async_copy(q_hbm, q_ref, loc_sem.at[0])
    q_copy.start()
    k_copy = pltpu.make_async_copy(k_hbm, kbuf.at[rank], loc_sem.at[1])
    k_copy.start()
    mass[...] = jnp.zeros_like(mass)
    pool[...] = jnp.zeros_like(pool)
    if safe:
        peak[...] = jnp.full_like(peak, NEG_FLOOR)
    k_copy.wait()
    pl.semaphore_wait(barrier, n_ctx + n_head - 2)

    def own_copy(to_chip):
        return pltpu.make_async_remote_copy(
            src_ref=kbuf.at[rank],
            dst_ref=kbuf.at[rank],
            send_sem=own_send.at[to_chip],
            recv_sem=key_recv.at[rank],
            device_id={"ctx": to_chip * 2 + core},
            device_id_type=MESH,
        )

    def sibling_copy(piece, sem):
        return pltpu.make_async_remote_copy(
            src_ref=kbuf.at[piece],
            dst_ref=kbuf.at[piece],
            send_sem=sem,
            recv_sem=key_recv.at[piece],
            device_id={"ctx": sibling},
            device_id_type=MESH,
        )

    @pl.when(core == 0)
    def _():
        sibling_copy(rank, own_send.at[chip]).start()

    @pl.loop(chip + 1, n_chip)
    def _(c):
        own_copy(c).start()

    q_copy.wait()

    def tile_sum(h, keys, row_low, row_count, mask):
        q = q_ref[pl.ds(row_low, row_count), pl.ds(pl.multiple_of(h * D_HEAD, D_HEAD), D_HEAD)]
        s = lax.dot_general(keys, q, NT, preferred_element_type=F32)
        if safe:
            shown = s if mask is None else jnp.where(mask, s, NEG_FLOOR)
            top = jnp.max(shown, axis=0, keepdims=True)
            s = s - top
        else:
            top = None
        p = jnp.exp2(s * EXP2_SCALE)
        if mask is not None:
            p = jnp.where(mask, p, 0.0)
        return jnp.sum(p, axis=0, keepdims=True), top

    def put(h, block, low, count, value):
        mass[h, pl.ds(block, 1), pl.ds(low, count)] = value[0]
        if safe:
            peak[h, pl.ds(block, 1), pl.ds(low, count)] = value[1]

    def pool_of(keys):
        return jnp.sum(keys.astype(F32), axis=0, keepdims=True) * (1.0 / BLOCK)

    own_block = rank * 2
    tri = lax.broadcasted_iota(jnp.int32, (BLOCK, BLOCK), 0) <= lax.broadcasted_iota(
        jnp.int32, (BLOCK, BLOCK), 1
    )

    def diagonal(h, _):
        first = kbuf[rank, :BLOCK]
        second = kbuf[rank, BLOCK:]
        put(h, own_block, 0, BLOCK, tile_sum(h, first, 0, BLOCK, tri))
        put(h, own_block, BLOCK, BLOCK, tile_sum(h, first, BLOCK, BLOCK, None))
        put(h, own_block + 1, BLOCK, BLOCK, tile_sum(h, second, BLOCK, BLOCK, tri))
        return 0

    pool[pl.ds(own_block, 1), :] = pool_of(kbuf[rank, :BLOCK])
    pool[pl.ds(own_block + 1, 1), :] = pool_of(kbuf[rank, BLOCK:])
    lax.fori_loop(0, GROUP, diagonal, 0)

    def piece_step(i, _):
        later = i - core
        back = 1 + later // 2
        phase = later % 2
        far = (chip - back) * 2 + jnp.where(phase == 0, core, 1 - core)
        piece = jnp.where(later < 0, rank - 1, far)
        sibling_copy(piece, own_send.at[chip]).wait_recv()

        @pl.when((later >= 0) & (phase == 0))
        def _():
            sibling_copy(piece, fwd_send.at[chip - back]).start()

        for half in range(2):
            keys = kbuf[piece, half * BLOCK : (half + 1) * BLOCK]
            pool[pl.ds(piece * 2 + half, 1), :] = pool_of(keys)
            for h in range(GROUP):
                put(h, piece * 2 + half, 0, rows, tile_sum(h, keys, 0, rows, None))
        return 0

    lax.fori_loop(0, rank, piece_step, 0)

    p1, p2, p3 = split3(pool[...])
    pool_rows = jnp.concatenate([p1, p2, p3], axis=0)
    pool_stack = jnp.concatenate([p1, p2, p3, p1, p2, p1], axis=0)
    block_id = lax.broadcasted_iota(jnp.int32, (n_block, rows), 0)
    row_block = own_block + lax.broadcasted_iota(jnp.int32, (n_block, rows), 1) // BLOCK
    allowed = block_id <= row_block
    grad_sum = jnp.zeros((n_block, D_HEAD), F32)
    entropy = jnp.zeros((1, rows), F32)
    bad = jnp.zeros((1, rows), F32)
    for h in range(GROUP):
        q = q_ref[:, h * D_HEAD : (h + 1) * D_HEAD]
        g3 = lax.dot_general(pool_rows, q, NT, preferred_element_type=F32)
        logits = (g3[2 * n_block :] + g3[n_block : 2 * n_block]) + g3[:n_block]
        m = mass[h]
        if safe:
            top = jnp.max(peak[h], axis=0, keepdims=True)
            m = m * jnp.exp2((peak[h] - top) * EXP2_SCALE)
        total = jnp.sum(m, axis=0, keepdims=True)
        fine = (total > TOTAL_LOW) & (total < TOTAL_HIGH)
        bad = bad + jnp.where(fine, 0.0, 1.0)
        teacher = m / total
        top = jnp.max(jnp.where(allowed, logits, NEG_FLOOR), axis=0, keepdims=True)
        weights = jnp.where(allowed, jnp.exp(logits - top), 0.0)
        weight_sum = jnp.sum(weights, axis=0, keepdims=True)
        student = weights / weight_sum
        entropy = entropy + (
            top + jnp.log(weight_sum) - jnp.sum(teacher * logits, axis=0, keepdims=True)
        )
        e1, e2, e3 = split3(student - teacher)
        three = jnp.concatenate([e1, e2, e3], axis=0)
        parts[h] = three
        g = lax.dot_general(three, q, NN, preferred_element_type=F32)
        grad_sum = grad_sum + ((g[2 * n_block :] + g[n_block : 2 * n_block]) + g[:n_block])

    grad_sum = grad_sum * (1.0 / BLOCK)
    lane_sum = lambda x: sum(x[:, i * 128 : (i + 1) * 128] for i in range(rows // 128))
    entropy_lanes = lane_sum(entropy)
    bad_lanes = lane_sum(bad)
    for t in range(n_ctx):
        gbs[t, 0:2, :] = grad_sum[2 * t : 2 * t + 2, :]
        gbs[t, 2:3, :] = entropy_lanes
        gbs[t, 3:4, :] = bad_lanes
        gbs[t, 4:8, :] = jnp.zeros((4, 128), F32)

    def r1_copy(slot, to):
        return pltpu.make_async_remote_copy(
            src_ref=gbs.at[to],
            dst_ref=gbr.at[slot],
            send_sem=r1_send.at[to],
            recv_sem=r1_recv.at[slot],
            device_id={"ctx": to},
            device_id_type=MESH,
        )

    @pl.loop(1, n_ctx)
    def _(o):
        r1_copy(rank, lax.rem(rank + o, n_ctx)).start()

    gbr[rank] = gbs[rank]

    def grad_rows(h):
        e1 = parts[h, :n_block]
        e2 = parts[h, n_block : 2 * n_block]
        e3 = parts[h, 2 * n_block :]
        stack = jnp.concatenate([e1, e1, e1, e2, e2, e3], axis=0)
        gq_ref[:, h * D_HEAD : (h + 1) * D_HEAD] = lax.dot_general(
            stack, pool_stack, TN, preferred_element_type=F32
        )

    for h in range(GROUP):
        grad_rows(h)

    @pl.loop(1, n_ctx)
    def _(o):
        other = lax.rem(rank + o, n_ctx)
        r1_copy(other, other).wait_recv()

    whole = gbr[0]
    for t in range(1, n_ctx):
        whole = whole + gbr[t]
    gb_ref[...] = whole[0:2]
    hsend[...] = whole

    def r2_copy(slot, to):
        return pltpu.make_async_remote_copy(
            src_ref=hsend,
            dst_ref=hrecv.at[slot],
            send_sem=r2_send.at[to],
            recv_sem=r2_recv.at[slot],
            device_id={"head": to},
            device_id_type=MESH,
        )

    @pl.loop(1, n_head)
    def _(o):
        r2_copy(head, lax.rem(head + o, n_head)).start()

    hrecv[head] = whole

    @pl.loop(1, n_ctx)
    def _(o):
        other = lax.rem(rank + o, n_ctx)
        r1_copy(rank, other).wait_send()

    @pl.when(core == 0)
    def _():
        sibling_copy(rank, own_send.at[chip]).wait_send()

    @pl.loop(chip + 1, n_chip)
    def _(c):
        own_copy(c).wait_send()

    @pl.loop(0, chip)
    def _(c):
        sibling_copy(rank, fwd_send.at[c]).wait_send()

    @pl.loop(1, n_head)
    def _(o):
        other = lax.rem(head + o, n_head)
        r2_copy(other, other).wait_recv()

    final = hrecv[0]
    for t in range(1, n_head):
        final = final + hrecv[t]
    st_ref[...] = jnp.broadcast_to(
        jnp.sum(final, axis=1, keepdims=True) * (1.0 / (rows * n_ctx * HEADS)), (8, 128)
    )

    @pl.loop(1, n_head)
    def _(o):
        other = lax.rem(head + o, n_head)
        r2_copy(head, other).wait_send()


def run(safe, n_ctx, n_head, queries, keys):
    rows = queries.shape[0]
    n_block = n_ctx * rows // BLOCK
    n_chip = n_ctx // 2
    dma = pltpu.SemaphoreType.DMA
    return pl.pallas_call(
        functools.partial(kernel, safe, n_ctx, n_head),
        out_shape=(
            jax.ShapeDtypeStruct((rows, GROUP * D_HEAD), F32),
            jax.ShapeDtypeStruct((rows // BLOCK, D_HEAD), F32),
            jax.ShapeDtypeStruct((8, 128), F32),
        ),
        in_specs=[pl.BlockSpec(memory_space=pl.ANY)] * 2,
        out_specs=(pl.BlockSpec(memory_space=pltpu.VMEM),) * 3,
        scratch_shapes=[
            pltpu.VMEM((rows, GROUP * D_HEAD), BF16),
            pltpu.VMEM((n_ctx, rows, D_HEAD), BF16),
            pltpu.VMEM((GROUP, n_block, rows), F32),
            pltpu.VMEM((GROUP, n_block, rows) if safe else (8, 128), F32),
            pltpu.VMEM((n_block, D_HEAD), F32),
            pltpu.VMEM((GROUP, 3 * n_block, rows), BF16),
            pltpu.VMEM((n_ctx, 8, 128), F32),
            pltpu.VMEM((n_ctx, 8, 128), F32),
            pltpu.VMEM((8, 128), F32),
            pltpu.VMEM((n_head, 8, 128), F32),
            dma((2,)),
            dma((n_chip,)),
            dma((n_chip,)),
            dma((n_ctx,)),
            dma((n_ctx,)),
            dma((n_ctx,)),
            dma((n_head,)),
            dma((n_head,)),
        ],
        compiler_params=pltpu.CompilerParams(
            collective_id=1 if safe else 0,
            has_side_effects=True,
            vmem_limit_bytes=48 * 1024 * 1024,
        ),
        name="gate_safe" if safe else "gate_fast",
    )(queries, keys)


def solution(mesh):
    n_ctx, n_head = mesh.shape["ctx"], mesh.shape["head"]

    def local(queries, keys):
        fast = run(False, n_ctx, n_head, queries, keys)
        ok = fast[2][3, 0] == 0.0
        out = lax.cond(
            ok,
            lambda: fast,
            lambda: run(True, n_ctx, n_head, queries, keys),
        )
        return out[0], out[1], out[2][2, 0]

    return jax.shard_map(
        local,
        mesh=mesh,
        in_specs=(P("ctx", "head"), P("ctx", "head")),
        out_specs=(P("ctx", "head"), P("ctx", "head"), P()),
        check_vma=False,
    )
```

time: 697 us -> 165 us (0.24)
  blocking collectives: 464 us -> 0 us
  Pallas kernels: 0 us -> 160 us
  loops' own time: 82.3 us -> 0.02 us
  other arithmetic: 52.7 us -> 0 us
  local copies, waits for them, and re-layouts: 46.8 us -> 2.91 us
  matrix products: 15.5 us -> 0 us
  between operations: 16.6 us -> 1.29 us
  waiting for transfers between devices: 12.9 us -> 0 us
    psum x1 -> x0, blocking collectives: 392 us -> none  [local(): loss = lax.psum(jnp.sum(cross_entropy), ('ctx', 'head')) / (seq_len * HEADS)]
    pallas_call x0 -> x2, Pallas kernels: none -> 160 us  [run(): pl.pallas_call(functools.partial(kernel, safe, n_ctx, n_head), out_shape=...]
    another operation x33 -> x1, loops' own time: 82.3 us -> 0.02 us  [local(): lax.cond(ok, lambda: fast, lambda: run(True, n_ctx, n_head, queries, keys))]
    unnamed x1 -> x0, blocking collectives: 49.9 us -> none
    all_gather x1 -> x0, blocking collectives: 22.3 us -> none  [local(): pooled = lax.all_gather(own_pooled, 'ctx', axis=0, tiled=True)]
    select_n x5 -> x0, other arithmetic: 19.1 us -> none  [the longest x4 19.1 us: advance_span(): jnp.where(causal_mask, jnp.exp(scores - new_peak[..., None]), 0.0)]
    reduce_sum x8 -> x0, other arithmetic: 18.6 us -> none  [the longest x4 16.7 us: advance_span(): jnp.sum(probability.reshape(span_shape[0], span_shape[1], span_shape[2],...]
    squeeze x16 -> x0, local copies, waits for them, and re-layouts: 15.6 us -> none  [local(): running, _ = lax.scan(absorb_part, running, (key_parts, part_starts))]
  transfers between devices with their start and end apart: 1 -> 0, of which waited for: 1 -> 0; matrix products, arithmetic and copies ran while one was open for 1% -> 0% of each run, Pallas kernels for 0% -> 0%
where the time goes in v1:
time: 165 us
  Pallas kernels  160 us (97%)
  local copies, waits for them, and re-layouts  2.91 us (2%)
    pallas_call x2, Pallas kernels, run(): pl.pallas_call(functools.partial(kernel, safe, n_ctx, n_head), out_shape=...  160 us

profile of v1, /device:TPU:1, one launch (start us, length us, event | category | flops | bytes accessed | tf_op | source)
XLA Modules:
  0.0 164.6 jit_solution(16395756475649913437)
XLA Ops:
  0.6 72.2 %gate_fast.1 = (f32[1024,512]{1,0:T(8,128)S(1)}, f32[2,128]{1,0:T(2,128)S(1)}, f32[8,128]{1,0:T(8,128)S(1)}) custom-call(bf16[1024,512]{1,0:T(8,128)(2,1)} %q_hbm.1, bf16[1024,128]{1,0:T(8,128)(2,1)} %k_hbm.1), custom_call_target="tpu_custom_call" | custom-call | tf_op jit(solution)/shard_map/gate_fast/pallas_call | solution.py:328
  72.8 0.5 slice.10
  74.0 88.8 %conditional.1 = (f32[1024,512]{1,0:T(8,128)S(1)}, f32[2,128]{1,0:T(2,128)S(1)}, f32[]{:T(128)}) conditional(s32[]{:T(128)} %bitcast.2, (bf16[1024,512]{1,0:T(8,128)(2,1)}, bf16[1024,128]{1,0:T(8,128)(2,1)}) %tuple.17, (f32[8,128]{1,0:T(8,128)S(1)}, f32[1024,512]{1,0:T(8,128)S(1)}, f32[2,128]{1,0:T(2,128)S(1)}) %tuple.18), branch_computations={%region_0.0_spmd, %region_1.0_spmd} | conditional | bytes 32 | solution.py:372
  74.0 88.3 %gate_safe.1 = (f32[1024,512]{1,0:T(8,128)S(1)}, f32[2,128]{1,0:T(2,128)S(1)}, f32[8,128]{1,0:T(8,128)S(1)}) custom-call(bf16[1024,512]{1,0:T(8,128)(2,1)} %get-tuple-element.17.q_hbm, bf16[1024,128]{1,0:T(8,128)(2,1)} %get-tuple-element.18.k_hbm), custom_call_target="tpu_custom_call" | custom-call | tf_op jit(solution)/shard_map/cond/branch_0_fun/gate_safe/pallas_call | solution.py:328
  162.2 0.5 slice.12
  162.8 1.3 copy.13
  164.1 0.6 copy.14

commit v2 on v1

--- a/solution.py
+++ b/solution.py
@@ -49,14 +49,20 @@
     peak,
     pool,
     parts,
+    ship_out,
+    ship_in,
     gbs,
     gbr,
     hsend,
     hrecv,
     loc_sem,
+    q_sem,
     own_send,
     fwd_send,
+    up_send,
     key_recv,
+    ship_send,
+    ship_recv,
     r1_send,
     r1_recv,
     r2_send,
@@ -64,12 +70,18 @@
 ):
     rank = lax.axis_index("ctx")
     head = lax.axis_index("head")
-    chip = rank // 2
-    core = rank % 2
-    sibling = chip * 2 + 1 - core
-    rows = q_ref.shape[0]
-    n_chip = n_ctx // 2
+    half_ctx = n_ctx // 2
+    n_z = half_ctx // 2
+    upper = rank // half_ctx
+    zee = lax.rem(rank, half_ctx) // 2
+    core = lax.rem(rank, 2)
+    plane = upper * half_ctx
+    sibling = plane + zee * 2 + 1 - core
+    partner = lax.rem(rank + half_ctx, n_ctx)
+    rows = mass.shape[2]
     n_block = mass.shape[1]
+    width = GROUP * D_HEAD
+    kept = width // 2
 
     barrier = pltpu.get_barrier_semaphore()
 
@@ -85,7 +97,7 @@
             barrier, inc=1, device_id={"head": lax.rem(head + o, n_head)}, device_id_type=MESH
         )
 
-    q_copy = pltpu.make_async_copy(q_hbm, q_ref, loc_sem.at[0])
+    q_copy = pltpu.make_async_copy(q_hbm, q_ref.at[:, :width], loc_sem.at[0])
     q_copy.start()
     k_copy = pltpu.make_async_copy(k_hbm, kbuf.at[rank], loc_sem.at[1])
     k_copy.start()
@@ -96,33 +108,48 @@
     k_copy.wait()
     pl.semaphore_wait(barrier, n_ctx + n_head - 2)
 
-    def own_copy(to_chip):
-        return pltpu.make_async_remote_copy(
-            src_ref=kbuf.at[rank],
-            dst_ref=kbuf.at[rank],
-            send_sem=own_send.at[to_chip],
-            recv_sem=key_recv.at[rank],
-            device_id={"ctx": to_chip * 2 + core},
-            device_id_type=MESH,
-        )
-
-    def sibling_copy(piece, sem):
+    def key_copy(piece, to, sem):
         return pltpu.make_async_remote_copy(
             src_ref=kbuf.at[piece],
             dst_ref=kbuf.at[piece],
             send_sem=sem,
             recv_sem=key_recv.at[piece],
-            device_id={"ctx": sibling},
+            device_id={"ctx": to},
             device_id_type=MESH,
         )
 
-    @pl.when(core == 0)
+    def own_across(o):
+        return key_copy(rank, plane + lax.rem(zee + o, n_z) * 2 + core, own_send.at[o])
+
+    own_sibling = key_copy(rank, sibling, own_send.at[0])
+    own_up = key_copy(rank, partner, own_send.at[n_z])
+    q_ship = pltpu.make_async_remote_copy(
+        src_ref=q_hbm.at[:, kept:],
+        dst_ref=q_ref.at[:, width:],
+        send_sem=q_sem.at[0],
+        recv_sem=q_sem.at[1],
+        device_id={"ctx": partner},
+        device_id_type=MESH,
+    )
+
+    @pl.when(upper == 0)
     def _():
-        sibling_copy(rank, own_send.at[chip]).start()
-
-    @pl.loop(chip + 1, n_chip)
-    def _(c):
-        own_copy(c).start()
+        own_sibling.start()
+        own_up.start()
+        for o in (n_z - 1, *range(1, n_z - 1)):
+            own_across(o).start()
+
+    @pl.when(upper == 1)
+    def _():
+        q_ship.start()
+
+        @pl.when(core == 0)
+        def _():
+            own_sibling.start()
+
+        @pl.loop(1, n_z - zee)
+        def _(o):
+            own_across(o).start()
 
     q_copy.wait()
 
@@ -165,26 +192,103 @@
     pool[pl.ds(own_block + 1, 1), :] = pool_of(kbuf[rank, BLOCK:])
     lax.fori_loop(0, GROUP, diagonal, 0)
 
-    def piece_step(i, _):
-        later = i - core
-        back = 1 + later // 2
-        phase = later % 2
-        far = (chip - back) * 2 + jnp.where(phase == 0, core, 1 - core)
-        piece = jnp.where(later < 0, rank - 1, far)
-        sibling_copy(piece, own_send.at[chip]).wait_recv()
-
-        @pl.when((later >= 0) & (phase == 0))
-        def _():
-            sibling_copy(piece, fwd_send.at[chip - back]).start()
-
-        for half in range(2):
-            keys = kbuf[piece, half * BLOCK : (half + 1) * BLOCK]
-            pool[pl.ds(piece * 2 + half, 1), :] = pool_of(keys)
-            for h in range(GROUP):
-                put(h, piece * 2 + half, 0, rows, tile_sum(h, keys, 0, rows, None))
+    def ship_copy(piece):
+        return pltpu.make_async_remote_copy(
+            src_ref=ship_out.at[piece],
+            dst_ref=ship_in.at[piece],
+            send_sem=ship_send.at[piece],
+            recv_sem=ship_recv.at[piece],
+            device_id={"ctx": partner},
+            device_id_type=MESH,
+        )
+
+    def arrival_z(o):
+        return lax.rem(zee + jnp.where(o == 1, n_z - 1, jnp.where(o == 0, 0, o - 1)), n_z)
+
+    n_low = half_ctx - 1 + half_ctx
+    n_up = core + 2 * zee + half_ctx
+    n_steps = jnp.where(upper == 0, n_low, n_up)
+
+    def step(i, _):
+        lo_phase = lax.rem(i + 1, 2)
+        lo_core = jnp.where(lo_phase == 0, core, 1 - core)
+        lo_piece = arrival_z((i + 1) // 2) * 2 + lo_core
+        lo_ship = i >= half_ctx - 1
+        lo_piece = jnp.where(lo_ship, i - (half_ctx - 1), lo_piece)
+        lo_direct = (lo_phase == 0) & (i < half_ctx - 1)
+        j = jnp.maximum(i - core, 0)
+        up_phase = lax.rem(j, 2)
+        up_core = jnp.where(up_phase == 0, core, 1 - core)
+        up_own = j < 2 * zee
+        up_z = jnp.where(up_own, zee - 1 - j // 2, arrival_z((j - 2 * zee) // 2))
+        up_piece = jnp.where(up_own, half_ctx, 0) + up_z * 2 + up_core
+        up_sib = i < core
+        up_piece = jnp.where(up_sib, rank - 1, up_piece)
+        up_direct = (up_phase == 0) & jnp.logical_not(up_sib)
+        low = upper == 0
+        piece = jnp.where(low, lo_piece, up_piece)
+        direct = jnp.where(low, lo_direct.astype(jnp.int32), up_direct.astype(jnp.int32)) == 1
+        shipped = low & lo_ship
+        full = jnp.where(low, jnp.where(lo_piece < rank, 2, 0), jnp.where(up_own | up_sib, 2, 1))
+        hp_low = jnp.where(shipped, 2, 0)
+        hp_high = jnp.where(shipped, 3, full)
+
+        @pl.when(jnp.logical_not(shipped))
+        def _():
+            key_copy(piece, sibling, own_send.at[0]).wait_recv()
+
+        @pl.when(direct)
+        def _():
+            key_copy(piece, sibling, fwd_send.at[piece]).start()
+
+        @pl.when(direct & low)
+        def _():
+            key_copy(piece, partner, up_send.at[piece]).start()
+
+        @pl.when(low & (i == half_ctx - 1))
+        def _():
+            q_ship.wait_recv()
+
+        def unit(hp, _):
+            for half in range(2):
+                keys = kbuf[piece, half * BLOCK : (half + 1) * BLOCK]
+                block = piece * 2 + half
+                pool[pl.ds(block, 1), :] = pool_of(keys)
+                for j in range(2):
+                    h = hp * 2 + j
+                    put(h, block, 0, rows, tile_sum(h, keys, 0, rows, None))
+            return 0
+
+        lax.fori_loop(hp_low, hp_high, unit, 0)
+
+        @pl.when(shipped)
+        def _():
+            for k, source in enumerate((mass, peak) if safe else (mass,)):
+                for j in range(2):
+                    for half in range(2):
+                        for part in range(2):
+                            ship_out[piece, k * 8 + j * 4 + half * 2 + part, :] = source[
+                                GROUP + j, piece * 2 + half, part * BLOCK : (part + 1) * BLOCK
+                            ]
+            ship_copy(piece).start()
+
         return 0
 
-    lax.fori_loop(0, rank, piece_step, 0)
+    lax.fori_loop(0, n_steps, step, 0)
+
+    def collect():
+        def one(piece, _):
+            ship_copy(piece).wait_recv()
+            for k, target in enumerate((mass, peak) if safe else (mass,)):
+                for j in range(2):
+                    for half in range(2):
+                        for part in range(2):
+                            target[
+                                2 + j, piece * 2 + half, part * BLOCK : (part + 1) * BLOCK
+                            ] = ship_in[piece, k * 8 + j * 4 + half * 2 + part, :]
+            return 0
+
+        lax.fori_loop(0, half_ctx, one, 0)
 
     p1, p2, p3 = split3(pool[...])
     pool_rows = jnp.concatenate([p1, p2, p3], axis=0)
@@ -196,6 +300,8 @@
     entropy = jnp.zeros((1, rows), F32)
     bad = jnp.zeros((1, rows), F32)
     for h in range(GROUP):
+        if h == 2:
+            pl.when(upper == 1)(collect)
         q = q_ref[:, h * D_HEAD : (h + 1) * D_HEAD]
         g3 = lax.dot_general(pool_rows, q, NT, preferred_element_type=F32)
         logits = (g3[2 * n_block :] + g3[n_block : 2 * n_block]) + g3[:n_block]
@@ -290,17 +396,38 @@
         other = lax.rem(rank + o, n_ctx)
         r1_copy(rank, other).wait_send()
 
-    @pl.when(core == 0)
+    @pl.when(upper == 0)
     def _():
-        sibling_copy(rank, own_send.at[chip]).wait_send()
-
-    @pl.loop(chip + 1, n_chip)
-    def _(c):
-        own_copy(c).wait_send()
-
-    @pl.loop(0, chip)
-    def _(c):
-        sibling_copy(rank, fwd_send.at[c]).wait_send()
+        own_sibling.wait_send()
+        own_up.wait_send()
+        for o in range(1, n_z):
+            own_across(o).wait_send()
+            piece = lax.rem(zee + o, n_z) * 2 + core
+            key_copy(piece, sibling, fwd_send.at[piece]).wait_send()
+            key_copy(piece, partner, up_send.at[piece]).wait_send()
+        for piece in range(half_ctx):
+            ship_copy(piece).wait_send()
+
+    @pl.when(upper == 1)
+    def _():
+        q_ship.wait_send()
+
+        @pl.when(core == 0)
+        def _():
+            own_sibling.wait_send()
+
+        @pl.loop(1, n_z - zee)
+        def _(o):
+            own_across(o).wait_send()
+
+        @pl.loop(0, zee)
+        def _(z):
+            piece = half_ctx + z * 2 + core
+            key_copy(piece, sibling, fwd_send.at[piece]).wait_send()
+
+        for z in range(n_z):
+            piece = z * 2 + core
+            key_copy(piece, sibling, fwd_send.at[piece]).wait_send()
 
     @pl.loop(1, n_head)
     def _(o):
@@ -323,7 +450,8 @@
 def run(safe, n_ctx, n_head, queries, keys):
     rows = queries.shape[0]
     n_block = n_ctx * rows // BLOCK
-    n_chip = n_ctx // 2
+    half_ctx = n_ctx // 2
+    ship_rows = 16 if safe else 8
     dma = pltpu.SemaphoreType.DMA
     return pl.pallas_call(
         functools.partial(kernel, safe, n_ctx, n_head),
@@ -335,20 +463,26 @@
         in_specs=[pl.BlockSpec(memory_space=pl.ANY)] * 2,
         out_specs=(pl.BlockSpec(memory_space=pltpu.VMEM),) * 3,
         scratch_shapes=[
-            pltpu.VMEM((rows, GROUP * D_HEAD), BF16),
+            pltpu.VMEM((rows, (GROUP + 2) * D_HEAD), BF16),
             pltpu.VMEM((n_ctx, rows, D_HEAD), BF16),
-            pltpu.VMEM((GROUP, n_block, rows), F32),
-            pltpu.VMEM((GROUP, n_block, rows) if safe else (8, 128), F32),
+            pltpu.VMEM((GROUP + 2, n_block, rows), F32),
+            pltpu.VMEM((GROUP + 2, n_block, rows) if safe else (8, 128), F32),
             pltpu.VMEM((n_block, D_HEAD), F32),
             pltpu.VMEM((GROUP, 3 * n_block, rows), BF16),
+            pltpu.VMEM((half_ctx, ship_rows, BLOCK), F32),
+            pltpu.VMEM((half_ctx, ship_rows, BLOCK), F32),
             pltpu.VMEM((n_ctx, 8, 128), F32),
             pltpu.VMEM((n_ctx, 8, 128), F32),
             pltpu.VMEM((8, 128), F32),
             pltpu.VMEM((n_head, 8, 128), F32),
             dma((2,)),
-            dma((n_chip,)),
-            dma((n_chip,)),
+            dma((2,)),
+            dma((half_ctx // 2 + 1,)),
             dma((n_ctx,)),
+            dma((half_ctx,)),
+            dma((n_ctx,)),
+            dma((half_ctx,)),
+            dma((half_ctx,)),
             dma((n_ctx,)),
             dma((n_ctx,)),
             dma((n_head,)),

time: 165 us -> 133 us (0.81)
  Pallas kernels: 160 us -> 129 us
    pallas_call x2, Pallas kernels: 160 us -> 129 us  [run(): pl.pallas_call(functools.partial(kernel, safe, n_ctx, n_head), out_shape=...]
where the time goes in v2:
time: 133 us
  Pallas kernels  129 us (97%)
  local copies, waits for them, and re-layouts  2.91 us (2%)
    pallas_call x2, Pallas kernels, run(): pl.pallas_call(functools.partial(kernel, safe, n_ctx, n_head), out_shape=...  129 us

profile of v2, /device:TPU:1, one launch (start us, length us, event | category | flops | bytes accessed | tf_op | source)
XLA Modules:
  0.0 133.2 jit_solution(16385978054217985228)
XLA Ops:
  0.6 55.1 %gate_fast.1 = (f32[1024,512]{1,0:T(8,128)S(1)}, f32[2,128]{1,0:T(2,128)S(1)}, f32[8,128]{1,0:T(8,128)S(1)}) custom-call(bf16[1024,512]{1,0:T(8,128)(2,1)} %q_hbm.1, bf16[1024,128]{1,0:T(8,128)(2,1)} %k_hbm.1), custom_call_target="tpu_custom_call" | custom-call | tf_op jit(solution)/shard_map/gate_fast/pallas_call | solution.py:456
  55.8 0.5 slice.10
  56.9 74.4 %conditional.1 = (f32[1024,512]{1,0:T(8,128)S(1)}, f32[2,128]{1,0:T(2,128)S(1)}, f32[]{:T(128)}) conditional(s32[]{:T(128)} %bitcast.2, (bf16[1024,512]{1,0:T(8,128)(2,1)}, bf16[1024,128]{1,0:T(8,128)(2,1)}) %tuple.17, (f32[8,128]{1,0:T(8,128)S(1)}, f32[1024,512]{1,0:T(8,128)S(1)}, f32[2,128]{1,0:T(2,128)S(1)}) %tuple.18), branch_computations={%region_0.0_spmd, %region_1.0_spmd} | conditional | bytes 32 | solution.py:506
  56.9 73.9 %gate_safe.1 = (f32[1024,512]{1,0:T(8,128)S(1)}, f32[2,128]{1,0:T(2,128)S(1)}, f32[8,128]{1,0:T(8,128)S(1)}) custom-call(bf16[1024,512]{1,0:T(8,128)(2,1)} %get-tuple-element.17.q_hbm, bf16[1024,128]{1,0:T(8,128)(2,1)} %get-tuple-element.18.k_hbm), custom_call_target="tpu_custom_call" | custom-call | tf_op jit(solution)/shard_map/cond/branch_0_fun/gate_safe/pallas_call | solution.py:456
  130.9 0.5 slice.12
  131.4 1.3 copy.13
  132.7 0.6 copy.14

commit v3 on v2

--- a/solution.py
+++ b/solution.py
@@ -42,7 +42,8 @@
     k_hbm,
     gq_ref,
     gb_ref,
-    st_ref,
+    loss_ref,
+    bad_ref,
     q_ref,
     kbuf,
     mass,
@@ -59,7 +60,8 @@
     q_sem,
     own_send,
     fwd_send,
-    up_send,
+    next_send,
+    prev_send,
     key_recv,
     ship_send,
     ship_recv,
@@ -118,11 +120,34 @@
             device_id_type=MESH,
         )
 
-    def own_across(o):
-        return key_copy(rank, plane + lax.rem(zee + o, n_z) * 2 + core, own_send.at[o])
-
+    z_next = lax.rem(zee + 1, n_z)
+    z_prev = lax.rem(zee + n_z - 1, n_z)
+    z_far = lax.rem(zee + 2, n_z)
+    to_next = plane + z_next * 2 + core
+    to_prev = plane + z_prev * 2 + core
     own_sibling = key_copy(rank, sibling, own_send.at[0])
-    own_up = key_copy(rank, partner, own_send.at[n_z])
+    own_next = key_copy(rank, to_next, own_send.at[1])
+    own_prev = key_copy(rank, to_prev, own_send.at[2])
+    own_up = key_copy(rank, partner, own_send.at[3])
+
+    def lower(z):
+        return z * 2 + core
+
+    def higher(z):
+        return half_ctx + z * 2 + core
+
+    def to_sibling(piece):
+        return key_copy(piece, sibling, fwd_send.at[piece])
+
+    def onward(piece):
+        return key_copy(piece, to_next, next_send.at[piece])
+
+    def backward(piece):
+        return key_copy(piece, to_prev, prev_send.at[piece])
+
+    def arrived(piece):
+        key_copy(piece, sibling, own_send.at[0]).wait_recv()
+
     q_ship = pltpu.make_async_remote_copy(
         src_ref=q_hbm.at[:, kept:],
         dst_ref=q_ref.at[:, width:],
@@ -134,22 +159,26 @@
 
     @pl.when(upper == 0)
     def _():
+        own_up.start()
+        own_prev.start()
+        own_next.start()
         own_sibling.start()
-        own_up.start()
-        for o in (n_z - 1, *range(1, n_z - 1)):
-            own_across(o).start()
 
     @pl.when(upper == 1)
     def _():
         q_ship.start()
 
+        @pl.when(zee < n_z - 1)
+        def _():
+            own_next.start()
+
+        @pl.when(zee == 0)
+        def _():
+            own_prev.start()
+
         @pl.when(core == 0)
         def _():
             own_sibling.start()
-
-        @pl.loop(1, n_z - zee)
-        def _(o):
-            own_across(o).start()
 
     q_copy.wait()
 
@@ -176,119 +205,186 @@
         return jnp.sum(keys.astype(F32), axis=0, keepdims=True) * (1.0 / BLOCK)
 
     own_block = rank * 2
-    tri = lax.broadcasted_iota(jnp.int32, (BLOCK, BLOCK), 0) <= lax.broadcasted_iota(
-        jnp.int32, (BLOCK, BLOCK), 1
+    sub = BLOCK // 2
+    tri_wide = lax.broadcasted_iota(jnp.int32, (sub, BLOCK), 0) <= lax.broadcasted_iota(
+        jnp.int32, (sub, BLOCK), 1
     )
-
-    def diagonal(h, _):
-        first = kbuf[rank, :BLOCK]
-        second = kbuf[rank, BLOCK:]
-        put(h, own_block, 0, BLOCK, tile_sum(h, first, 0, BLOCK, tri))
+    tri = tri_wide[:, :sub]
+
+    def diagonal(h, keys, block, low):
+        early = tile_sum(h, keys[:sub], low, BLOCK, tri_wide)
+        late = tile_sum(h, keys[sub:], low + sub, sub, tri)
+        put(h, block, low, sub, tuple(None if x is None else x[:, :sub] for x in early))
+        both = early[0][:, sub:] + late[0]
+        top = early[1]
+        if safe:
+            top = jnp.maximum(early[1][:, sub:], late[1])
+            both = early[0][:, sub:] * jnp.exp2((early[1][:, sub:] - top) * EXP2_SCALE) + late[
+                0
+            ] * jnp.exp2((late[1] - top) * EXP2_SCALE)
+        put(h, block, low + sub, sub, (both, top))
+
+    first = kbuf[rank, :BLOCK]
+    second = kbuf[rank, BLOCK:]
+    pool[pl.ds(own_block, 1), :] = pool_of(first)
+    pool[pl.ds(own_block + 1, 1), :] = pool_of(second)
+    for h in range(GROUP):
+        diagonal(h, first, own_block, 0)
         put(h, own_block, BLOCK, BLOCK, tile_sum(h, first, BLOCK, BLOCK, None))
-        put(h, own_block + 1, BLOCK, BLOCK, tile_sum(h, second, BLOCK, BLOCK, tri))
-        return 0
-
-    pool[pl.ds(own_block, 1), :] = pool_of(kbuf[rank, :BLOCK])
-    pool[pl.ds(own_block + 1, 1), :] = pool_of(kbuf[rank, BLOCK:])
-    lax.fori_loop(0, GROUP, diagonal, 0)
-
-    def ship_copy(piece):
+        diagonal(h, second, own_block + 1, BLOCK)
+
+    def ship_copy(z):
         return pltpu.make_async_remote_copy(
-            src_ref=ship_out.at[piece],
-            dst_ref=ship_in.at[piece],
-            send_sem=ship_send.at[piece],
-            recv_sem=ship_recv.at[piece],
+            src_ref=ship_out.at[z],
+            dst_ref=ship_in.at[z],
+            send_sem=ship_send.at[z],
+            recv_sem=ship_recv.at[z],
             device_id={"ctx": partner},
             device_id_type=MESH,
         )
 
-    def arrival_z(o):
-        return lax.rem(zee + jnp.where(o == 1, n_z - 1, jnp.where(o == 0, 0, o - 1)), n_z)
-
-    n_low = half_ctx - 1 + half_ctx
-    n_up = core + 2 * zee + half_ctx
-    n_steps = jnp.where(upper == 0, n_low, n_up)
+    def pick(i, values):
+        out = values[-1]
+        for n in range(len(values) - 2, -1, -1):
+            out = jnp.where(i == n, values[n], out)
+        return out
+
+    shapes = [(j, blk, part) for j in range(2) for blk in range(4) for part in range(2)]
+    kept_state = (mass, peak) if safe else (mass,)
+    n_steps = 11
 
     def step(i, _):
-        lo_phase = lax.rem(i + 1, 2)
-        lo_core = jnp.where(lo_phase == 0, core, 1 - core)
-        lo_piece = arrival_z((i + 1) // 2) * 2 + lo_core
-        lo_ship = i >= half_ctx - 1
-        lo_piece = jnp.where(lo_ship, i - (half_ctx - 1), lo_piece)
-        lo_direct = (lo_phase == 0) & (i < half_ctx - 1)
-        j = jnp.maximum(i - core, 0)
-        up_phase = lax.rem(j, 2)
-        up_core = jnp.where(up_phase == 0, core, 1 - core)
-        up_own = j < 2 * zee
-        up_z = jnp.where(up_own, zee - 1 - j // 2, arrival_z((j - 2 * zee) // 2))
-        up_piece = jnp.where(up_own, half_ctx, 0) + up_z * 2 + up_core
-        up_sib = i < core
-        up_piece = jnp.where(up_sib, rank - 1, up_piece)
-        up_direct = (up_phase == 0) & jnp.logical_not(up_sib)
         low = upper == 0
-        piece = jnp.where(low, lo_piece, up_piece)
-        direct = jnp.where(low, lo_direct.astype(jnp.int32), up_direct.astype(jnp.int32)) == 1
-        shipped = low & lo_ship
-        full = jnp.where(low, jnp.where(lo_piece < rank, 2, 0), jnp.where(up_own | up_sib, 2, 1))
-        hp_low = jnp.where(shipped, 2, 0)
-        hp_high = jnp.where(shipped, 3, full)
-
-        @pl.when(jnp.logical_not(shipped))
-        def _():
-            key_copy(piece, sibling, own_send.at[0]).wait_recv()
-
-        @pl.when(direct)
-        def _():
-            key_copy(piece, sibling, fwd_send.at[piece]).start()
-
-        @pl.when(direct & low)
-        def _():
-            key_copy(piece, partner, up_send.at[piece]).start()
-
-        @pl.when(low & (i == half_ctx - 1))
+        high = upper == 1
+
+        @pl.when(low & (i == 1))
+        def _():
+            arrived(lower(z_next))
+            backward(lower(z_next)).start()
+            to_sibling(lower(z_next)).start()
+            arrived(lower(z_prev))
+            to_sibling(lower(z_prev)).start()
+
+        @pl.when(low & (i == 5))
         def _():
             q_ship.wait_recv()
 
-        def unit(hp, _):
+        @pl.when(low & (i == 7))
+        def _():
+            arrived(lower(z_far))
+            to_sibling(lower(z_far)).start()
+
+        @pl.when(high & (i == 1))
+        def _():
+            @pl.when(zee > 0)
+            def _():
+                arrived(higher(z_prev))
+
+                @pl.when(zee < n_z - 1)
+                def _():
+                    onward(higher(z_prev)).start()
+
+                to_sibling(higher(z_prev)).start()
+
+            arrived(lower(zee))
+            backward(lower(zee)).start()
+            onward(lower(zee)).start()
+            to_sibling(lower(zee)).start()
+
+        @pl.when(high & (i == 3) & (zee == n_z - 1))
+        def _():
+            arrived(higher(0))
+            to_sibling(higher(0)).start()
+
+        @pl.when(high & (i == 5))
+        def _():
+            arrived(lower(z_next))
+            backward(lower(z_next)).start()
+            to_sibling(lower(z_next)).start()
+
+            @pl.when(zee >= 2)
+            def _():
+                arrived(higher(z_far))
+                to_sibling(higher(z_far)).start()
+
+        @pl.when(high & (i == 7))
+        def _():
+            arrived(lower(z_prev))
+            to_sibling(lower(z_prev)).start()
+
+        @pl.when(high & (i == 9))
+        def _():
+            arrived(lower(z_far))
+            to_sibling(lower(z_far)).start()
+
+        phase = lax.rem(i + 1, 2)
+        narrow = jnp.where(low, (i < 5) | (i > 8), i < 7)
+        lo_z = pick(
+            i, (zee, z_prev, z_prev, z_next, z_next, zee, z_prev, z_next, z_far, z_far, z_far)
+        )
+        hi_z = pick(i, (zee, z_prev, z_prev, 0, 0, z_far, z_far, zee, z_prev, z_next, z_far))
+        here = jnp.where(low, lo_z, hi_z)
+        lo_side = jnp.where(i == 9, core, 1 - core)
+        side = jnp.where(phase == 0, core, 1 - core)
+        side = jnp.where(low & (i > 8), lo_side, side)
+        piece = jnp.where(high & narrow, half_ctx, 0) + here * 2 + side
+        least = pick(i, (0, 1, 1, 3, 3, 2, 2, 0, 0, 0, 0))
+        live = jnp.where(
+            low,
+            piece < rank,
+            jnp.where(i == 0, core == 1, zee >= least),
+        )
+        lo_wait = (i == 0) | (i == 2) | (i == 4) | (i == 8)
+        hi_wait = (i >= 7) | (live & (phase == 1))
+        wait = jnp.where(low, lo_wait, hi_wait)
+
+        @pl.when(wait)
+        def _():
+            arrived(jnp.where(narrow, piece, here * 2 + 1 - core))
+
+        @pl.when(narrow & live)
+        def _():
             for half in range(2):
                 keys = kbuf[piece, half * BLOCK : (half + 1) * BLOCK]
                 block = piece * 2 + half
                 pool[pl.ds(block, 1), :] = pool_of(keys)
+                for h in range(GROUP):
+                    put(h, block, 0, rows, tile_sum(h, keys, 0, rows, None))
+
+        @pl.when(jnp.logical_not(narrow))
+        def _():
+            base = jnp.where(low, GROUP, 0)
+            for blk in range(4):
+                keys = kbuf[here * 2 + blk // 2, blk % 2 * BLOCK : (blk % 2 + 1) * BLOCK]
+                block = here * 4 + blk
+                pool[pl.ds(block, 1), :] = pool_of(keys)
                 for j in range(2):
-                    h = hp * 2 + j
-                    put(h, block, 0, rows, tile_sum(h, keys, 0, rows, None))
+                    put(base + j, block, 0, rows, tile_sum(base + j, keys, 0, rows, None))
+
+        @pl.when(low & jnp.logical_not(narrow))
+        def _():
+            for k, source in enumerate(kept_state):
+                for n, (j, blk, part) in enumerate(shapes):
+                    ship_out[here, k * 16 + n, :] = source[
+                        GROUP + j, here * 4 + blk, part * BLOCK : (part + 1) * BLOCK
+                    ]
+            ship_copy(here).start()
+
+        return 0
+
+    lax.fori_loop(0, n_steps, step, 0)
+
+    def collect():
+        def one(z, _):
+            ship_copy(z).wait_recv()
+            for k, target in enumerate(kept_state):
+                for n, (j, blk, part) in enumerate(shapes):
+                    target[2 + j, z * 4 + blk, part * BLOCK : (part + 1) * BLOCK] = ship_in[
+                        z, k * 16 + n, :
+                    ]
             return 0
 
-        lax.fori_loop(hp_low, hp_high, unit, 0)
-
-        @pl.when(shipped)
-        def _():
-            for k, source in enumerate((mass, peak) if safe else (mass,)):
-                for j in range(2):
-                    for half in range(2):
-                        for part in range(2):
-                            ship_out[piece, k * 8 + j * 4 + half * 2 + part, :] = source[
-                                GROUP + j, piece * 2 + half, part * BLOCK : (part + 1) * BLOCK
-                            ]
-            ship_copy(piece).start()
-
-        return 0
-
-    lax.fori_loop(0, n_steps, step, 0)
-
-    def collect():
-        def one(piece, _):
-            ship_copy(piece).wait_recv()
-            for k, target in enumerate((mass, peak) if safe else (mass,)):
-                for j in range(2):
-                    for half in range(2):
-                        for part in range(2):
-                            target[
-                                2 + j, piece * 2 + half, part * BLOCK : (part + 1) * BLOCK
-                            ] = ship_in[piece, k * 8 + j * 4 + half * 2 + part, :]
-            return 0
-
-        lax.fori_loop(0, half_ctx, one, 0)
+        lax.fori_loop(0, n_z, one, 0)
 
     p1, p2, p3 = split3(pool[...])
     pool_rows = jnp.concatenate([p1, p2, p3], axis=0)
@@ -398,36 +494,42 @@
 
     @pl.when(upper == 0)
     def _():
-        own_sibling.wait_send()
-        own_up.wait_send()
-        for o in range(1, n_z):
-            own_across(o).wait_send()
-            piece = lax.rem(zee + o, n_z) * 2 + core
-            key_copy(piece, sibling, fwd_send.at[piece]).wait_send()
-            key_copy(piece, partner, up_send.at[piece]).wait_send()
-        for piece in range(half_ctx):
-            ship_copy(piece).wait_send()
+        for own in (own_sibling, own_next, own_prev, own_up):
+            own.wait_send()
+        backward(lower(z_next)).wait_send()
+        for z in (z_prev, z_next, z_far):
+            to_sibling(lower(z)).wait_send()
+        for z in range(n_z):
+            ship_copy(z).wait_send()
 
     @pl.when(upper == 1)
     def _():
         q_ship.wait_send()
+        backward(lower(zee)).wait_send()
+        onward(lower(zee)).wait_send()
+        backward(lower(z_next)).wait_send()
+        for z in range(n_z):
+            to_sibling(lower(z)).wait_send()
 
         @pl.when(core == 0)
         def _():
             own_sibling.wait_send()
 
-        @pl.loop(1, n_z - zee)
-        def _(o):
-            own_across(o).wait_send()
+        @pl.when(zee < n_z - 1)
+        def _():
+            own_next.wait_send()
+
+        @pl.when(zee == 0)
+        def _():
+            own_prev.wait_send()
+
+        @pl.when((zee > 0) & (zee < n_z - 1))
+        def _():
+            onward(higher(z_prev)).wait_send()
 
         @pl.loop(0, zee)
         def _(z):
-            piece = half_ctx + z * 2 + core
-            key_copy(piece, sibling, fwd_send.at[piece]).wait_send()
-
-        for z in range(n_z):
-            piece = z * 2 + core
-            key_copy(piece, sibling, fwd_send.at[piece]).wait_send()
+            to_sibling(higher(z)).wait_send()
 
     @pl.loop(1, n_head)
     def _(o):
@@ -437,9 +539,9 @@
     final = hrecv[0]
     for t in range(1, n_head):
         final = final + hrecv[t]
-    st_ref[...] = jnp.broadcast_to(
-        jnp.sum(final, axis=1, keepdims=True) * (1.0 / (rows * n_ctx * HEADS)), (8, 128)
-    )
+    sums = jnp.sum(final, axis=1, keepdims=True)
+    loss_ref[...] = sums[2:3] * (1.0 / (rows * n_ctx * HEADS))
+    bad_ref[...] = sums[3:4]
 
     @pl.loop(1, n_head)
     def _(o):
@@ -451,17 +553,18 @@
     rows = queries.shape[0]
     n_block = n_ctx * rows // BLOCK
     half_ctx = n_ctx // 2
-    ship_rows = 16 if safe else 8
+    ship_rows = 32 if safe else 16
     dma = pltpu.SemaphoreType.DMA
     return pl.pallas_call(
         functools.partial(kernel, safe, n_ctx, n_head),
         out_shape=(
             jax.ShapeDtypeStruct((rows, GROUP * D_HEAD), F32),
             jax.ShapeDtypeStruct((rows // BLOCK, D_HEAD), F32),
-            jax.ShapeDtypeStruct((8, 128), F32),
+            jax.ShapeDtypeStruct((1, 1), F32),
+            jax.ShapeDtypeStruct((1, 1), F32),
         ),
         in_specs=[pl.BlockSpec(memory_space=pl.ANY)] * 2,
-        out_specs=(pl.BlockSpec(memory_space=pltpu.VMEM),) * 3,
+        out_specs=(pl.BlockSpec(memory_space=pltpu.VMEM),) * 4,
         scratch_shapes=[
             pltpu.VMEM((rows, (GROUP + 2) * D_HEAD), BF16),
             pltpu.VMEM((n_ctx, rows, D_HEAD), BF16),
@@ -469,17 +572,18 @@
             pltpu.VMEM((GROUP + 2, n_block, rows) if safe else (8, 128), F32),
             pltpu.VMEM((n_block, D_HEAD), F32),
             pltpu.VMEM((GROUP, 3 * n_block, rows), BF16),
-            pltpu.VMEM((half_ctx, ship_rows, BLOCK), F32),
-            pltpu.VMEM((half_ctx, ship_rows, BLOCK), F32),
+            pltpu.VMEM((half_ctx // 2, ship_rows, BLOCK), F32),
+            pltpu.VMEM((half_ctx // 2, ship_rows, BLOCK), F32),
             pltpu.VMEM((n_ctx, 8, 128), F32),
             pltpu.VMEM((n_ctx, 8, 128), F32),
             pltpu.VMEM((8, 128), F32),
             pltpu.VMEM((n_head, 8, 128), F32),
             dma((2,)),
             dma((2,)),
-            dma((half_ctx // 2 + 1,)),
+            dma((4,)),
             dma((n_ctx,)),
-            dma((half_ctx,)),
+            dma((n_ctx,)),
+            dma((n_ctx,)),
             dma((n_ctx,)),
             dma((half_ctx,)),
             dma((half_ctx,)),
@@ -502,13 +606,13 @@
 
     def local(queries, keys):
         fast = run(False, n_ctx, n_head, queries, keys)
-        ok = fast[2][3, 0] == 0.0
+        ok = fast[3].reshape(()) == 0.0
         out = lax.cond(
             ok,
-            lambda: fast,
-            lambda: run(True, n_ctx, n_head, queries, keys),
-        )
-        return out[0], out[1], out[2][2, 0]
+            lambda: fast[:3],
+            lambda: run(True, n_ctx, n_head, queries, keys)[:3],
+        )
+        return out[0], out[1], out[2].reshape(())
 
     return jax.shard_map(
         local,

time: 133 us -> 129 us (0.970)
  Pallas kernels: 129 us -> 123 us
  between operations: 1.29 us -> 2.95 us
    pallas_call x2, Pallas kernels: 129 us -> 123 us  [run(): pl.pallas_call(functools.partial(kernel, safe, n_ctx, n_head), out_shape=...]
where the time goes in v3:
time: 129 us; the launch traced here: 128 us
  Pallas kernels  123 us (95%)
  between operations  2.95 us (2%)
  local copies, waits for them, and re-layouts  1.88 us (1%)
    pallas_call x2, Pallas kernels, run(): pl.pallas_call(functools.partial(kernel, safe, n_ctx, n_head), out_shape=...  123 us

profile of v3, /device:TPU:1, one launch (start us, length us, event | category | flops | bytes accessed | tf_op | source)
XLA Modules:
  0.0 128.4 jit_solution(9298199461750485910)
XLA Ops:
  0.6 53.3 %gate_fast.1 = (f32[1024,512]{1,0:T(8,128)S(1)}, f32[2,128]{1,0:T(2,128)S(1)}, f32[1,1]{1,0:T(1,128)}, f32[1,1]{1,0:T(1,128)}) custom-call(bf16[1024,512]{1,0:T(8,128)(2,1)} %q_hbm.1, bf16[1024,128]{1,0:T(8,128)(2,1)} %k_hbm.1), custom_call_target="tpu_custom_call" | custom-call | tf_op jit(solution)/shard_map/gate_fast/pallas_call | solution.py:558
  54.5 70.3 %conditional.1 = ((f32[1024,512]{1,0:T(8,128)S(1)}, f32[2,128]{1,0:T(2,128)S(1)}, f32[1,1]{1,0:T(1,128)})) conditional(s32[]{:T(128)} %bitcast, (bf16[1024,512]{1,0:T(8,128)(2,1)}, bf16[1024,128]{1,0:T(8,128)(2,1)}) %tuple.15, (f32[1024,512]{1,0:T(8,128)S(1)}, f32[2,128]{1,0:T(2,128)S(1)}, f32[1,1]{1,0:T(1,128)}) %tuple.16), branch_computations={%region_0.0_spmd, %region_1.0_spmd} | conditional | bytes 32 | solution.py:610
  54.7 69.9 %gate_safe.1 = (f32[1024,512]{1,0:T(8,128)S(1)}, f32[2,128]{1,0:T(2,128)S(1)}, f32[1,1]{1,0:T(1,128)}, f32[1,1]{1,0:T(1,128)}) custom-call(bf16[1024,512]{1,0:T(8,128)(2,1)} %get-tuple-element.10.q_hbm, bf16[1024,128]{1,0:T(8,128)(2,1)} %get-tuple-element.11.k_hbm), custom_call_target="tpu_custom_call" | custom-call | tf_op jit(solution)/shard_map/cond/branch_0_fun/gate_safe/pallas_call | solution.py:558
  124.8 1.3 %copy.14 = f32[1024,512]{1,0:T(8,128)} copy(f32[1024,512]{1,0:T(8,128)S(1)} %get-tuple-element.41) | data formatting | bytes 4194304
  126.1 0.6 copy.15

commit v4 on v3

--- a/solution.py
+++ b/solution.py
@@ -65,6 +65,7 @@
     key_recv,
     ship_send,
     ship_recv,
+    zq_sem,
     r1_send,
     r1_recv,
     r2_send,
@@ -150,12 +151,28 @@
 
     q_ship = pltpu.make_async_remote_copy(
         src_ref=q_hbm.at[:, kept:],
-        dst_ref=q_ref.at[:, width:],
+        dst_ref=q_ref.at[:, width : width + kept],
         send_sem=q_sem.at[0],
         recv_sem=q_sem.at[1],
         device_id={"ctx": partner},
         device_id_type=MESH,
     )
+
+    z_mate = plane + (n_z - 1 - zee) * 2 + core
+    z_first = zee == 0
+    z_last = zee == n_z - 1
+    zq_ship = pltpu.make_async_remote_copy(
+        src_ref=q_hbm.at[:, kept:],
+        dst_ref=q_ref.at[:, width + kept :],
+        send_sem=zq_sem.at[0],
+        recv_sem=zq_sem.at[1],
+        device_id={"ctx": z_mate},
+        device_id_type=MESH,
+    )
+
+    @pl.when(z_last)
+    def _():
+        zq_ship.start()
 
     @pl.when(upper == 0)
     def _():
@@ -172,11 +189,11 @@
         def _():
             own_next.start()
 
-        @pl.when(zee == 0)
+        @pl.when(zee <= 1)
         def _():
             own_prev.start()
 
-        @pl.when(core == 0)
+        @pl.when((core == 0) | z_first)
         def _():
             own_sibling.start()
 
@@ -239,7 +256,7 @@
             dst_ref=ship_in.at[z],
             send_sem=ship_send.at[z],
             recv_sem=ship_recv.at[z],
-            device_id={"ctx": partner},
+            device_id={"ctx": jnp.where(z < n_z, partner, z_mate)},
             device_id_type=MESH,
         )
 
@@ -251,96 +268,173 @@
 
     shapes = [(j, blk, part) for j in range(2) for blk in range(4) for part in range(2)]
     kept_state = (mass, peak) if safe else (mass,)
-    n_steps = 11
+    n_steps = 9
+
+    def lower_sib(z):
+        return z * 2 + 1 - core
+
+    def higher_sib(z):
+        return half_ctx + z * 2 + 1 - core
 
     def step(i, _):
         low = upper == 0
         high = upper == 1
 
-        @pl.when(low & (i == 1))
-        def _():
-            arrived(lower(z_next))
-            backward(lower(z_next)).start()
-            to_sibling(lower(z_next)).start()
-            arrived(lower(z_prev))
-            to_sibling(lower(z_prev)).start()
-
-        @pl.when(low & (i == 5))
-        def _():
-            q_ship.wait_recv()
-
-        @pl.when(low & (i == 7))
-        def _():
-            arrived(lower(z_far))
-            to_sibling(lower(z_far)).start()
-
-        @pl.when(high & (i == 1))
-        def _():
-            @pl.when(zee > 0)
-            def _():
-                arrived(higher(z_prev))
-
-                @pl.when(zee < n_z - 1)
+        @pl.when(low)
+        def _():
+            @pl.when(i == 0)
+            def _():
+                arrived(sibling)
+
+            @pl.when(i == 1)
+            def _():
+                arrived(lower(z_next))
+                backward(lower(z_next)).start()
+                to_sibling(lower(z_next)).start()
+
+            @pl.when(i == jnp.where(z_first, 6, 1))
+            def _():
+                arrived(lower(z_prev))
+                to_sibling(lower(z_prev)).start()
+
+            @pl.when(i == jnp.where(z_first, 7, 2))
+            def _():
+                arrived(lower_sib(z_prev))
+
+            @pl.when(i == 3)
+            def _():
+                arrived(lower_sib(z_next))
+
+            @pl.when(i == jnp.where(z_last, 4, 3))
+            def _():
+                q_ship.wait_recv()
+
+            @pl.when(i == 4)
+            def _():
+                arrived(lower(z_far))
+                to_sibling(lower(z_far)).start()
+
+            @pl.when(i == 5)
+            def _():
+                arrived(lower_sib(z_far))
+
+        @pl.when(high)
+        def _():
+            @pl.when((i == 0) & (core == 1))
+            def _():
+                arrived(sibling)
+
+            @pl.when(i == 1)
+            def _():
+                @pl.when(zee > 0)
                 def _():
-                    onward(higher(z_prev)).start()
-
-                to_sibling(higher(z_prev)).start()
-
-            arrived(lower(zee))
-            backward(lower(zee)).start()
-            onward(lower(zee)).start()
-            to_sibling(lower(zee)).start()
-
-        @pl.when(high & (i == 3) & (zee == n_z - 1))
-        def _():
-            arrived(higher(0))
-            to_sibling(higher(0)).start()
-
-        @pl.when(high & (i == 5))
-        def _():
-            arrived(lower(z_next))
-            backward(lower(z_next)).start()
-            to_sibling(lower(z_next)).start()
-
-            @pl.when(zee >= 2)
-            def _():
-                arrived(higher(z_far))
-                to_sibling(higher(z_far)).start()
-
-        @pl.when(high & (i == 7))
-        def _():
-            arrived(lower(z_prev))
-            to_sibling(lower(z_prev)).start()
-
-        @pl.when(high & (i == 9))
-        def _():
-            arrived(lower(z_far))
-            to_sibling(lower(z_far)).start()
-
-        phase = lax.rem(i + 1, 2)
-        narrow = jnp.where(low, (i < 5) | (i > 8), i < 7)
-        lo_z = pick(
-            i, (zee, z_prev, z_prev, z_next, z_next, zee, z_prev, z_next, z_far, z_far, z_far)
-        )
-        hi_z = pick(i, (zee, z_prev, z_prev, 0, 0, z_far, z_far, zee, z_prev, z_next, z_far))
-        here = jnp.where(low, lo_z, hi_z)
-        lo_side = jnp.where(i == 9, core, 1 - core)
-        side = jnp.where(phase == 0, core, 1 - core)
-        side = jnp.where(low & (i > 8), lo_side, side)
-        piece = jnp.where(high & narrow, half_ctx, 0) + here * 2 + side
-        least = pick(i, (0, 1, 1, 3, 3, 2, 2, 0, 0, 0, 0))
+                    arrived(higher(z_prev))
+
+                    @pl.when(zee < n_z - 1)
+                    def _():
+                        onward(higher(z_prev)).start()
+
+                    to_sibling(higher(z_prev)).start()
+
+                arrived(lower(zee))
+                backward(lower(zee)).start()
+                onward(lower(zee)).start()
+                to_sibling(lower(zee)).start()
+
+            @pl.when((i == 2) & (zee > 0))
+            def _():
+                arrived(higher_sib(z_prev))
+
+            @pl.when((i == 2) & z_last)
+            def _():
+                arrived(higher(0))
+                to_sibling(higher(0)).start()
+
+            @pl.when(i == 3)
+            def _():
+                arrived(lower_sib(zee))
+
+                @pl.when(z_last)
+                def _():
+                    arrived(higher_sib(0))
+
+            @pl.when(i == 4)
+            def _():
+                arrived(lower(z_next))
+                backward(lower(z_next)).start()
+                to_sibling(lower(z_next)).start()
+
+                @pl.when(zee >= 2)
+                def _():
+                    arrived(higher(z_far))
+                    to_sibling(higher(z_far)).start()
+
+                @pl.when(z_first)
+                def _():
+                    arrived(higher(1))
+                    to_sibling(higher(1)).start()
+
+            @pl.when((i == 5) & (zee >= 2))
+            def _():
+                arrived(higher_sib(z_far))
+
+            @pl.when(i == 6)
+            def _():
+                arrived(lower_sib(z_next))
+                arrived(lower(z_prev))
+                to_sibling(lower(z_prev)).start()
+
+            @pl.when(i == 7)
+            def _():
+                arrived(lower_sib(z_prev))
+                arrived(lower(z_far))
+                to_sibling(lower(z_far)).start()
+
+            @pl.when(i == 8)
+            def _():
+                arrived(lower_sib(z_far))
+
+            @pl.when((i == 4) & z_first & (core == 0))
+            def _():
+                arrived(sibling)
+
+            @pl.when((i == 5) & z_first)
+            def _():
+                arrived(higher_sib(1))
+
+        @pl.when((i == 4) & z_first)
+        def _():
+            zq_ship.wait_recv()
+
+        narrow = (i <= 2) | ((zee == n_z - 2) & ((i == 4) | (i == 5)))
+        side = jnp.where((i == 1) | (i == 4), core, 1 - core)
+        piece = plane + pick(i, (zee, z_prev, z_prev, 0)) * 2 + side
+        z_turn = z_first & ((i == 4) | (i == 5))
+        own_turn = jnp.where(low, 8, 5)
+        in_plane = z_turn | (z_last & ((i == 3) | (i == own_turn)))
+        here = pick(
+            i,
+            (
+                0,
+                0,
+                0,
+                jnp.where(z_last, 0, zee),
+                jnp.where(z_first, 0, zee),
+                1,
+                z_next,
+                z_prev,
+                z_far,
+            ),
+        )
+        first_piece = jnp.where(in_plane, plane, 0) + here * 2
+        base = jnp.where(
+            z_turn, GROUP + 2, jnp.where(low & jnp.logical_not(in_plane), GROUP, 0)
+        )
         live = jnp.where(
-            low,
-            piece < rank,
-            jnp.where(i == 0, core == 1, zee >= least),
-        )
-        lo_wait = (i == 0) | (i == 2) | (i == 4) | (i == 8)
-        hi_wait = (i >= 7) | (live & (phase == 1))
-        wait = jnp.where(low, lo_wait, hi_wait)
-
-        @pl.when(wait)
-        def _():
-            arrived(jnp.where(narrow, piece, here * 2 + 1 - core))
+            i == 0,
+            core == 1,
+            (zee >= pick(i, (0, 1, 1, 0, 2, 2, 0, 0, 0))) | z_turn,
+        )
 
         @pl.when(narrow & live)
         def _():
@@ -351,40 +445,42 @@
                 for h in range(GROUP):
                     put(h, block, 0, rows, tile_sum(h, keys, 0, rows, None))
 
-        @pl.when(jnp.logical_not(narrow))
-        def _():
-            base = jnp.where(low, GROUP, 0)
+        @pl.when(jnp.logical_not(narrow) & live)
+        def _():
             for blk in range(4):
-                keys = kbuf[here * 2 + blk // 2, blk % 2 * BLOCK : (blk % 2 + 1) * BLOCK]
-                block = here * 4 + blk
+                keys = kbuf[first_piece + blk // 2, blk % 2 * BLOCK : (blk % 2 + 1) * BLOCK]
+                block = first_piece * 2 + blk
                 pool[pl.ds(block, 1), :] = pool_of(keys)
                 for j in range(2):
                     put(base + j, block, 0, rows, tile_sum(base + j, keys, 0, rows, None))
 
-        @pl.when(low & jnp.logical_not(narrow))
-        def _():
+        @pl.when(live & jnp.logical_not(narrow) & (base > 0))
+        def _():
+            slot = jnp.where(z_turn, n_z, 0) + here
             for k, source in enumerate(kept_state):
                 for n, (j, blk, part) in enumerate(shapes):
-                    ship_out[here, k * 16 + n, :] = source[
-                        GROUP + j, here * 4 + blk, part * BLOCK : (part + 1) * BLOCK
+                    ship_out[slot, k * 16 + n, :] = source[
+                        base + j, first_piece * 2 + blk, part * BLOCK : (part + 1) * BLOCK
                     ]
-            ship_copy(here).start()
+            ship_copy(slot).start()
 
         return 0
 
     lax.fori_loop(0, n_steps, step, 0)
 
-    def collect():
+    def collect(low_slot, high_slot, first_block):
         def one(z, _):
             ship_copy(z).wait_recv()
             for k, target in enumerate(kept_state):
                 for n, (j, blk, part) in enumerate(shapes):
-                    target[2 + j, z * 4 + blk, part * BLOCK : (part + 1) * BLOCK] = ship_in[
-                        z, k * 16 + n, :
-                    ]
+                    target[
+                        2 + j,
+                        first_block + (z - low_slot) * 4 + blk,
+                        part * BLOCK : (part + 1) * BLOCK,
+                    ] = ship_in[z, k * 16 + n, :]
             return 0
 
-        lax.fori_loop(0, n_z, one, 0)
+        lax.fori_loop(low_slot, high_slot, one, 0)
 
     p1, p2, p3 = split3(pool[...])
     pool_rows = jnp.concatenate([p1, p2, p3], axis=0)
@@ -397,7 +493,8 @@
     bad = jnp.zeros((1, rows), F32)
     for h in range(GROUP):
         if h == 2:
-            pl.when(upper == 1)(collect)
+            pl.when(upper == 1)(functools.partial(collect, 0, n_z, 0))
+            pl.when(z_last)(functools.partial(collect, n_z, n_z + 2, plane * 2))
         q = q_ref[:, h * D_HEAD : (h + 1) * D_HEAD]
         g3 = lax.dot_general(pool_rows, q, NT, preferred_element_type=F32)
         logits = (g3[2 * n_block :] + g3[n_block : 2 * n_block]) + g3[:n_block]
@@ -489,8 +586,7 @@
 
     @pl.loop(1, n_ctx)
     def _(o):
-        other = lax.rem(rank + o, n_ctx)
-        r1_copy(rank, other).wait_send()
+        r1_copy(rank, lax.rem(rank + o, n_ctx)).wait_send()
 
     @pl.when(upper == 0)
     def _():
@@ -511,7 +607,7 @@
         for z in range(n_z):
             to_sibling(lower(z)).wait_send()
 
-        @pl.when(core == 0)
+        @pl.when((core == 0) | z_first)
         def _():
             own_sibling.wait_send()
 
@@ -519,9 +615,13 @@
         def _():
             own_next.wait_send()
 
-        @pl.when(zee == 0)
+        @pl.when(zee <= 1)
         def _():
             own_prev.wait_send()
+
+        @pl.when(z_first)
+        def _():
+            to_sibling(higher(1)).wait_send()
 
         @pl.when((zee > 0) & (zee < n_z - 1))
         def _():
@@ -530,6 +630,15 @@
         @pl.loop(0, zee)
         def _(z):
             to_sibling(higher(z)).wait_send()
+
+    @pl.when(z_last)
+    def _():
+        zq_ship.wait_send()
+
+    @pl.when(z_first)
+    def _():
+        for z in range(n_z, n_z + 2):
+            ship_copy(z).wait_send()
 
     @pl.loop(1, n_head)
     def _(o):
@@ -566,14 +675,14 @@
         in_specs=[pl.BlockSpec(memory_space=pl.ANY)] * 2,
         out_specs=(pl.BlockSpec(memory_space=pltpu.VMEM),) * 4,
         scratch_shapes=[
-            pltpu.VMEM((rows, (GROUP + 2) * D_HEAD), BF16),
+            pltpu.VMEM((rows, (GROUP + 4) * D_HEAD), BF16),
             pltpu.VMEM((n_ctx, rows, D_HEAD), BF16),
-            pltpu.VMEM((GROUP + 2, n_block, rows), F32),
-            pltpu.VMEM((GROUP + 2, n_block, rows) if safe else (8, 128), F32),
+            pltpu.VMEM((GROUP + 4, n_block, rows), F32),
+            pltpu.VMEM((GROUP + 4, n_block, rows) if safe else (8, 128), F32),
             pltpu.VMEM((n_block, D_HEAD), F32),
             pltpu.VMEM((GROUP, 3 * n_block, rows), BF16),
-            pltpu.VMEM((half_ctx // 2, ship_rows, BLOCK), F32),
-            pltpu.VMEM((half_ctx // 2, ship_rows, BLOCK), F32),
+            pltpu.VMEM((half_ctx // 2 + 2, ship_rows, BLOCK), F32),
+            pltpu.VMEM((half_ctx // 2 + 2, ship_rows, BLOCK), F32),
             pltpu.VMEM((n_ctx, 8, 128), F32),
             pltpu.VMEM((n_ctx, 8, 128), F32),
             pltpu.VMEM((8, 128), F32),
@@ -587,6 +696,7 @@
             dma((n_ctx,)),
             dma((half_ctx,)),
             dma((half_ctx,)),
+            dma((2,)),
             dma((n_ctx,)),
             dma((n_ctx,)),
             dma((n_head,)),

time: 129 us -> 120 us (0.930)
  Pallas kernels: 123 us -> 115 us
    pallas_call x2, Pallas kernels: 123 us -> 115 us  [run(): pl.pallas_call(functools.partial(kernel, safe, n_ctx, n_head), out_shape=...]
where the time goes in v4:
time: 120 us
  Pallas kernels  115 us (96%)
  between operations  2.95 us (2%)
  local copies, waits for them, and re-layouts  1.88 us (2%)
    pallas_call x2, Pallas kernels, run(): pl.pallas_call(functools.partial(kernel, safe, n_ctx, n_head), out_shape=...  115 us

profile of v4, /device:TPU:1, one launch (start us, length us, event | category | flops | bytes accessed | tf_op | source)
XLA Modules:
  0.0 120.2 jit_solution(14656599999908263035)
XLA Ops:
  0.6 50.4 %gate_fast.1 = (f32[1024,512]{1,0:T(8,128)S(1)}, f32[2,128]{1,0:T(2,128)S(1)}, f32[1,1]{1,0:T(1,128)}, f32[1,1]{1,0:T(1,128)}) custom-call(bf16[1024,512]{1,0:T(8,128)(2,1)} %q_hbm.1, bf16[1024,128]{1,0:T(8,128)(2,1)} %k_hbm.1), custom_call_target="tpu_custom_call" | custom-call | tf_op jit(solution)/shard_map/gate_fast/pallas_call | solution.py:667
  51.6 64.9 %conditional.1 = ((f32[1024,512]{1,0:T(8,128)S(1)}, f32[2,128]{1,0:T(2,128)S(1)}, f32[1,1]{1,0:T(1,128)})) conditional(s32[]{:T(128)} %bitcast, (bf16[1024,512]{1,0:T(8,128)(2,1)}, bf16[1024,128]{1,0:T(8,128)(2,1)}) %tuple.15, (f32[1024,512]{1,0:T(8,128)S(1)}, f32[2,128]{1,0:T(2,128)S(1)}, f32[1,1]{1,0:T(1,128)}) %tuple.16), branch_computations={%region_0.0_spmd, %region_1.0_spmd} | conditional | bytes 32 | solution.py:720
  51.8 64.5 %gate_safe.1 = (f32[1024,512]{1,0:T(8,128)S(1)}, f32[2,128]{1,0:T(2,128)S(1)}, f32[1,1]{1,0:T(1,128)}, f32[1,1]{1,0:T(1,128)}) custom-call(bf16[1024,512]{1,0:T(8,128)(2,1)} %get-tuple-element.10.q_hbm, bf16[1024,128]{1,0:T(8,128)(2,1)} %get-tuple-element.11.k_hbm), custom_call_target="tpu_custom_call" | custom-call | tf_op jit(solution)/shard_map/cond/branch_0_fun/gate_safe/pallas_call | solution.py:667
  116.6 1.3 %copy.14 = f32[1024,512]{1,0:T(8,128)} copy(f32[1024,512]{1,0:T(8,128)S(1)} %get-tuple-element.41) | data formatting | bytes 4194304
  117.9 0.6 copy.15

commit v5 on v4

--- a/solution.py
+++ b/solution.py
@@ -493,8 +493,8 @@
     bad = jnp.zeros((1, rows), F32)
     for h in range(GROUP):
         if h == 2:
+            pl.when(z_last)(functools.partial(collect, n_z, n_z + 2, plane * 2))
             pl.when(upper == 1)(functools.partial(collect, 0, n_z, 0))
-            pl.when(z_last)(functools.partial(collect, n_z, n_z + 2, plane * 2))
         q = q_ref[:, h * D_HEAD : (h + 1) * D_HEAD]
         g3 = lax.dot_general(pool_rows, q, NT, preferred_element_type=F32)
         logits = (g3[2 * n_block :] + g3[n_block : 2 * n_block]) + g3[:n_block]

time: 120 us -> 120 us (level)
  no operation moved by 1% of the time
where the time goes in v5:
time: 120 us
  Pallas kernels  115 us (96%)
  between operations  2.95 us (2%)
  local copies, waits for them, and re-layouts  1.88 us (2%)
    pallas_call x2, Pallas kernels, run(): pl.pallas_call(functools.partial(kernel, safe, n_ctx, n_head), out_shape=...  115 us

profile of v5, /device:TPU:1, one launch (start us, length us, event | category | flops | bytes accessed | tf_op | source)
XLA Modules:
  0.0 120.1 jit_solution(8909072367761833925)
XLA Ops:
  0.6 50.4 %gate_fast.1 = (f32[1024,512]{1,0:T(8,128)S(1)}, f32[2,128]{1,0:T(2,128)S(1)}, f32[1,1]{1,0:T(1,128)}, f32[1,1]{1,0:T(1,128)}) custom-call(bf16[1024,512]{1,0:T(8,128)(2,1)} %q_hbm.1, bf16[1024,128]{1,0:T(8,128)(2,1)} %k_hbm.1), custom_call_target="tpu_custom_call" | custom-call | tf_op jit(solution)/shard_map/gate_fast/pallas_call | solution.py:667
  51.6 64.9 %conditional.1 = ((f32[1024,512]{1,0:T(8,128)S(1)}, f32[2,128]{1,0:T(2,128)S(1)}, f32[1,1]{1,0:T(1,128)})) conditional(s32[]{:T(128)} %bitcast, (bf16[1024,512]{1,0:T(8,128)(2,1)}, bf16[1024,128]{1,0:T(8,128)(2,1)}) %tuple.15, (f32[1024,512]{1,0:T(8,128)S(1)}, f32[2,128]{1,0:T(2,128)S(1)}, f32[1,1]{1,0:T(1,128)}) %tuple.16), branch_computations={%region_0.0_spmd, %region_1.0_spmd} | conditional | bytes 32 | solution.py:720
  51.8 64.4 %gate_safe.1 = (f32[1024,512]{1,0:T(8,128)S(1)}, f32[2,128]{1,0:T(2,128)S(1)}, f32[1,1]{1,0:T(1,128)}, f32[1,1]{1,0:T(1,128)}) custom-call(bf16[1024,512]{1,0:T(8,128)(2,1)} %get-tuple-element.10.q_hbm, bf16[1024,128]{1,0:T(8,128)(2,1)} %get-tuple-element.11.k_hbm), custom_call_target="tpu_custom_call" | custom-call | tf_op jit(solution)/shard_map/cond/branch_0_fun/gate_safe/pallas_call | solution.py:667
  116.5 1.3 %copy.14 = f32[1024,512]{1,0:T(8,128)} copy(f32[1024,512]{1,0:T(8,128)S(1)} %get-tuple-element.41) | data formatting | bytes 4194304
  117.8 0.6 copy.15
